TPU v7x, 256 devices: a whole 4x4x8 slice. The times are simulated.
256 devices in a mesh: tm: 32 (over z, x), fsdp: 8 (over y, core).
Axes of the slice: x: 4, y: 4, z: 8, core: 2. Of those that a mesh axis runs over, the one named last changes fastest.
Arguments:
- frames: bfloat16 [64, 64, 256, 128], P('tm', None, 'fsdp'), may hold values from -6 to 6
- conv_weight: bfloat16 [3, 3, 3, 128, 128], P(None, None, None, None, 'fsdp'), may hold values from -0.109375 to 0.109375
- mix_weight: bfloat16 [3, 128, 128], P(None, None, 'fsdp'), may hold values from -0.3125 to 0.3125
- cotangent: bfloat16 [32, 64, 256, 128], P(None, 'tm', 'fsdp'), may hold values from -0.008239746 to 0.008239746
Outputs:
- encoded: bfloat16 [32, 64, 256, 128], P(None, 'tm', 'fsdp')
- mix_grad: float32 [49152], P(('tm', 'fsdp'))
All inputs are finite; a program needn't handle non-finite values.
Results may differ from a plain program's by a relative error of at most 0.0058.
Values may be sent and summed in bfloat16 or wider, within the bound.
A program may use at most 64 MiB of HBM per device.

v0:
```python
import jax
import jax.numpy as jnp
from jax import lax
from jax.sharding import PartitionSpec as P


def from_behind(block, axis, distance):
    devices = range(lax.axis_size(axis))
    route = [(i - distance, i) for i in devices if i - distance in devices]
    return lax.ppermute(block, axis, route)


def with_halo(cells, sides, width):
    for axis, dim in sides:
        count = lax.axis_size(axis)
        ends = count - 1
        head = lax.slice_in_dim(cells, 0, width, axis=dim)
        tail = lax.slice_in_dim(cells, cells.shape[dim] - width, cells.shape[dim], axis=dim)
        cells = jnp.concatenate(
            [
                lax.ppermute(tail, axis, [(i, (i + 1) % count) for i in range(ends)]),
                cells,
                lax.ppermute(head, axis, [((i + 1) % count, i) for i in range(ends)]),
            ],
            axis=dim,
        )
    return cells


def pool_pairs(hidden):
    shaped = hidden.reshape((hidden.shape[0] // 2, 2) + hidden.shape[1:]).astype(jnp.float32)
    return ((shaped[:, 0] + shaped[:, 1]) * 0.5).astype(jnp.bfloat16)


def delayed(block, offset):
    return jnp.pad(block, ((offset, 0), (0, 0), (0, 0), (0, 0)))[: block.shape[0]]


def local(frames, conv_weight, mix_weight, cotangent):
    full_conv, full_mix = (
        lax.all_gather(conv_weight, "fsdp", axis=4, tiled=True),
        lax.all_gather(mix_weight, "fsdp", axis=2, tiled=True),
    )
    count_frames, height, width, channels = frames.shape
    previous = from_behind(frames, "tm", 1)
    timed = jnp.concatenate([previous, frames], axis=0)
    padded = with_halo(timed, (("fsdp", 2),), 1)
    padded = jnp.pad(padded, ((0, 0), (1, 1), (0, 0), (0, 0)))
    accum = jnp.zeros((count_frames * height * width, channels), jnp.float32)
    for row_tap in range(3):
        for col_tap in range(3):
            stacked = jnp.concatenate(
                [
                    padded[
                        step : step + count_frames,
                        row_tap : row_tap + height,
                        col_tap : col_tap + width,
                        :,
                    ]
                    for step in range(3)
                ],
                axis=3,
            ).reshape(-1, 3 * channels)
            kernel = full_conv[:, row_tap, col_tap].reshape(3 * channels, channels)
            accum = accum + jnp.dot(stacked, kernel, preferred_element_type=jnp.float32)
    hidden = jax.nn.silu(accum).astype(jnp.bfloat16).reshape(count_frames, height, width, channels)
    pooled = lax.all_to_all(pool_pairs(hidden), "tm", split_axis=1, concat_axis=0, tiled=True)
    branch = pooled.astype(jnp.float32).reshape(-1, channels)
    flat_cot = cotangent.reshape(-1, channels)
    grad_terms = []
    for offset in range(3):
        lagged = delayed(pooled, offset).reshape(-1, channels)
        branch = branch + jnp.dot(lagged, full_mix[offset], preferred_element_type=jnp.float32)
        grad_terms.append(
            lax.dot_general(
                lagged, flat_cot, (((0,), (0,)), ((), ())), preferred_element_type=jnp.float32
            )
        )
    encoded = branch.astype(jnp.bfloat16).reshape(pooled.shape)
    parts = lax.axis_size("tm") * lax.axis_size("fsdp")
    mix_grad = lax.all_to_all(
        jnp.stack(grad_terms).reshape(parts, -1), ("tm", "fsdp"), 0, 0, tiled=True
    ).sum(0)
    return (encoded, mix_grad)


def solution(mesh):
    return jax.shard_map(
        local,
        mesh=mesh,
        in_specs=(
            P("tm", None, "fsdp", None),
            P(None, None, None, None, "fsdp"),
            P(None, None, "fsdp"),
            P(None, "tm", "fsdp", None),
        ),
        out_specs=(P(None, "tm", "fsdp", None), P(("tm", "fsdp"))),
        check_vma=False,
    )
```

profile of v0, /device:TPU:1, one launch (start us, length us, event | category | flops | bytes accessed | tf_op | source)
XLA Modules:
  0.0 129.5 jit_solution(5271844698895392121)
XLA Ops:
  0.7 4.1 %collective-permute-start = (bf16[2,64,32,128]{3,2,1,0:T(8,128)(2,1)}, bf16[2,64,32,128]{3,2,1,0:T(8,128)(2,1)S(1)}, u32[]{:S(2)}, u32[]{:S(2)}) collective-permute-start(bf16[2,64,32,128]{3,2,1,0:T(8,128)(2,1)} %param.4), channel_id=1, source_target_pairs={{0,8},{8,16},{16,24},{24,32},{32,40},{40,48},{48,56},{56,64},{64,7... | collective-permute-start | bytes 3145736 | tf_op jit(solution)/shard_map/ppermute | solution.py:10
  4.8 15.0 %all_gather.6 = bf16[3,3,3,128,128]{3,4,2,1,0:T(8,128)(2,1)S(1)} all-gather(bf16[3,3,3,128,16]{3,4,2,1,0:T(8,128)(2,1)} %param.5), channel_id=1, replica_groups=mesh['tm'=32,'fsdp'=8] {'fsdp'}, dimensions={4}, use_global_device_ids=true | all-gather | bytes 995328 | tf_op jit(solution)/shard_map/all_gather | solution.py:41
  19.8 7.0 %collective-permute-done = bf16[2,64,32,128]{3,2,1,0:T(8,128)(2,1)S(1)} collective-permute-done((bf16[2,64,32,128]{3,2,1,0:T(8,128)(2,1)}, bf16[2,64,32,128]{3,2,1,0:T(8,128)(2,1)S(1)}, u32[]{:S(2)}, u32[]{:S(2)}) %collective-permute-start) | collective-permute-done | bytes 1048608 | tf_op jit(solution)/shard_map/ppermute | solution.py:10
  28.0 3.4 %collective-permute-start.2 = (bf16[4,64,1,128]{3,2,1,0:T(2,128)(2,1)}, bf16[4,64,1,128]{3,2,1,0:T(2,128)(2,1)S(1)}, u32[]{:S(2)}, u32[]{:S(2)}) collective-permute-start(bf16[4,64,1,128]{3,2,1,0:T(2,128)(2,1)} %get-tuple-element.30), channel_id=1, source_target_pairs={{1,0},{2,1},{3,2},{4,3},{5,4},{6,5},{7,6},{9,8},{10,9},{11,10},{12... | collective-permute-start | bytes 196616 | tf_op jit(solution)/shard_map/ppermute | solution.py:23
  31.5 3.1 %collective-permute-start.1 = (bf16[4,64,1,128]{3,2,1,0:T(2,128)(2,1)}, bf16[4,64,1,128]{3,2,1,0:T(2,128)(2,1)S(1)}, u32[]{:S(2)}, u32[]{:S(2)}) collective-permute-start(bf16[4,64,1,128]{3,2,1,0:T(2,128)(2,1)} %get-tuple-element.29), channel_id=1, source_target_pairs={{0,1},{1,2},{2,3},{3,4},{4,5},{5,6},{6,7},{8,9},{9,10},{10,11},{11... | collective-permute-start | bytes 196616 | tf_op jit(solution)/shard_map/ppermute | solution.py:21
  35.3 1.6 %copy.19 = bf16[3,1,1,128,128]{4,3,0,2,1:T(8,128)(2,1)} copy(bf16[3,1,1,128,128]{3,4,2,1,0:T(8,128)(2,1)} %get-tuple-element.39) | data formatting | bytes 196608
  39.4 1.6 %copy.27 = bf16[3,1,1,128,128]{4,3,0,2,1:T(8,128)(2,1)} copy(bf16[3,1,1,128,128]{3,4,2,1,0:T(8,128)(2,1)} %get-tuple-element.31) | data formatting | bytes 196608
  41.1 1.5 %fusion.7 = bf16[4,66,34,128]{3,2,1,0:T(8,128)(2,1)S(1)} fusion(bf16[4,64,1,128]{3,2,1,0:T(2,128)(2,1)S(1)} %collective-permute-done.2, bf16[4,64,32,128]{3,2,1,0:T(8,128)(2,1)S(1)} %constant_dynamic-update-slice_fusion, bf16[4,64,1,128]{3,2,1,0:T(2,128)(2,1)S(1)} %collective-permute-done.1), kind=kLoop, calls=%fused_computation.30 | loop fusion | flops 13787136 | bytes 4526080 | tf_op jit(solution)/shard_map/concatenate | solution.py:19
  42.6 6.9 %fusion.16 = (bf16[2,64,32,128]{3,2,1,0:T(8,128)(2,1)S(1)}, bf16[2,64,32,128]{3,2,1,0:T(8,128)(2,1)S(1)}, bf16[2,64,32,128]{3,2,1,0:T(8,128)(2,1)S(1)}, bf16[2,6...) fusion(bf16[4,66,34,128]{3,2,1,0:T(8,128)(2,1)S(1)} %fusion.7), kind=kLoop, calls=%fused_computation.59 | loop fusion | bytes 37748736 | tf_op jit(solution)/shard_map/slice | solution.py:54
  49.5 3.3 %pad_maximum_fusion.2 = (bf16[2,64,32,384]{3,2,1,0:T(8,128)(2,1)S(1)}, bf16[2,64,32,384]{3,2,1,0:T(8,128)(2,1)S(1)}) fusion(bf16[2,64,32,128]{3,2,1,0:T(8,128)(2,1)} %get-tuple-element.16, bf16[2,64,32,128]{3,2,1,0:T(8,128)(2,1)} %get-tuple-element.17, bf16[2,64,32,128]{3,2,1,0:T(8,128)(2,1)} %get-tuple-element.18, ...), kind=kLoop, calls=%fused_computation.19 | loop fusion | flops 18874368 | bytes 12582912 | tf_op jit(solution)/shard_map/concatenate | solution.py:52
  53.9 1.1 convolution_add_fusion.7
  57.8 2.1 %fusion.10 = (bf16[2,64,32,128]{3,2,1,0:T(8,128)(2,1)S(1)}, bf16[2,64,32,128]{3,2,1,0:T(8,128)(2,1)S(1)}, bf16[2,64,32,128]{3,2,1,0:T(8,128)(2,1)S(1)}, bf16[2,6...) fusion(bf16[4,64,32,128]{3,2,1,0:T(8,128)(2,1)S(1)} %constant_dynamic-update-slice_fusion, ...), kind=kLoop, calls=%fused_computation.44 | loop fusion | flops 8388608 | bytes 8650752 | tf_op jit(solution)/shard_map/concatenate | solution.py:19
  60.0 2.5 %fusion.1 = (bf16[2,64,32,384]{3,2,1,0:T(8,128)(2,1)S(1)}, bf16[2,64,32,384]{3,2,1,0:T(8,128)(2,1)S(1)}) fusion(bf16[4,64,1,128]{3,2,1,0:T(2,128)(2,1)S(1)} %collective-permute-done.2, bf16[4,64,32,128]{3,2,1,0:T(8,128)(2,1)S(1)} %constant_dynamic-update-slice_fusion, bf16[2,64,32,128]{3,2,1,0:T(8,128)(2,1)S(1)} %get-tuple-element.21, ...), kind=kLoop, calls=%fused_computation.16 | loop fusion | flops 25165824 | bytes 12713984 | tf_op jit(solution)/shard_map/concatenate | solution.py:52
  66.5 1.0 convolution_add_fusion.2
  68.4 1.0 convolution_add_fusion.1
  69.5 1.1 multiply_convert_fusion
  70.9 1.0 fusion.15
  71.9 12.8 %all-to-all-start = ((bf16[1,64,32,128]{3,2,0,1:T(8,128)(2,1)}), bf16[1,64,32,128]{3,2,0,1:T(8,128)(2,1)S(1)}, u32[]{:S(2)}, u32[]{:S(2)}) async-start(bf16[1,64,32,128]{3,2,0,1:T(8,128)(2,1)} %fusion.15), calls=%async_computation | async-start | bytes 1048576 | tf_op jit(solution)/shard_map/all_to_all | solution.py:67
  84.8 12.7 %all_gather.7 = bf16[3,128,128]{1,2,0:T(8,128)(2,1)S(1)} all-gather(bf16[3,128,16]{1,2,0:T(8,128)(2,1)S(1)} %copy-done.12), channel_id=1, replica_groups=mesh['tm'=32,'fsdp'=8] {'fsdp'}, dimensions={2}, use_global_device_ids=true | all-gather | bytes 110592 | tf_op jit(solution)/shard_map/all_gather | solution.py:42
  97.4 4.7 %all-to-all-done = bf16[1,64,32,128]{3,2,0,1:T(8,128)(2,1)S(1)} async-done(((bf16[1,64,32,128]{3,2,0,1:T(8,128)(2,1)}), bf16[1,64,32,128]{3,2,0,1:T(8,128)(2,1)S(1)}, u32[]{:S(2)}, u32[]{:S(2)}) %all-to-all-start) | async-done | bytes 524320 | tf_op jit(solution)/shard_map/all_to_all | solution.py:67
  103.7 1.1 all_to_all.22
  104.9 8.5 %all-to-all-start.1 = ((f32[256,1,192]{2,1,0:T(1,128)}), f32[256,1,192]{2,1,0:T(1,128)S(1)}, u32[]{:S(2)}, u32[]{:S(2)}) async-start(f32[256,1,192]{2,1,0:T(1,128)} %all_to_all.22), calls=%async_computation.1 | async-start | bytes 524288 | tf_op jit(solution)/shard_map/all_to_all | solution.py:81
  113.7 1.1 fusion.8
  114.8 13.9 %all-to-all-done.1 = f32[256,1,192]{2,1,0:T(1,128)S(1)} async-done(((f32[256,1,192]{2,1,0:T(1,128)}), f32[256,1,192]{2,1,0:T(1,128)S(1)}, u32[]{:S(2)}, u32[]{:S(2)}) %all-to-all-start.1) | async-done | bytes 196640 | tf_op jit(solution)/shard_map/all_to_all | solution.py:81
  (56 shorter events, 16.0 us)
Async XLA Ops:
  0.6 101.7 %copy-start = (bf16[32,2,32,128]{3,2,1,0:T(8,128)(2,1)S(1)}, bf16[32,2,32,128]{3,2,1,0:T(8,128)(2,1)}, u32[]{:S(2)}) copy-start(bf16[32,2,32,128]{3,2,1,0:T(8,128)(2,1)} %param.7) | copy-start | bytes 1572868
  0.6 26.3 %copy-start.5 = (bf16[2,64,32,128]{3,2,1,0:T(8,128)(2,1)S(1)}, bf16[2,64,32,128]{3,2,1,0:T(8,128)(2,1)}, u32[]{:S(2)}) copy-start(bf16[2,64,32,128]{3,2,1,0:T(8,128)(2,1)} %param.4) | copy-start | bytes 3145732
  0.7 26.2 %collective-permute-start = (bf16[2,64,32,128]{3,2,1,0:T(8,128)(2,1)}, bf16[2,64,32,128]{3,2,1,0:T(8,128)(2,1)S(1)}, u32[]{:S(2)}, u32[]{:S(2)}) collective-permute-start(bf16[2,64,32,128]{3,2,1,0:T(8,128)(2,1)} %param.4), channel_id=1, source_target_pairs={{0,8},{8,16},{16,24},{24,32},{32,40},{40,48},{48,56},{56,64},{64,7... | collective-permute-start | bytes 3145736 | tf_op jit(solution)/shard_map/ppermute | solution.py:10
  26.9 8.5 %copy-start.7 = (bf16[2,64,32,128]{3,2,1,0:T(8,128)(2,1)}, bf16[2,64,32,128]{3,2,1,0:T(8,128)(2,1)S(1)}, u32[]{:S(2)}) copy-start(bf16[2,64,32,128]{3,2,1,0:T(8,128)(2,1)S(1)} %collective-permute-done) | copy-start | bytes 3145732
  28.0 13.0 %collective-permute-start.2 = (bf16[4,64,1,128]{3,2,1,0:T(2,128)(2,1)}, bf16[4,64,1,128]{3,2,1,0:T(2,128)(2,1)S(1)}, u32[]{:S(2)}, u32[]{:S(2)}) collective-permute-start(bf16[4,64,1,128]{3,2,1,0:T(2,128)(2,1)} %get-tuple-element.30), channel_id=1, source_target_pairs={{1,0},{2,1},{3,2},{4,3},{5,4},{6,5},{7,6},{9,8},{10,9},{11,10},{12... | collective-permute-start | bytes 196616 | tf_op jit(solution)/shard_map/ppermute | solution.py:23
  31.5 9.6 %collective-permute-start.1 = (bf16[4,64,1,128]{3,2,1,0:T(2,128)(2,1)}, bf16[4,64,1,128]{3,2,1,0:T(2,128)(2,1)S(1)}, u32[]{:S(2)}, u32[]{:S(2)}) collective-permute-start(bf16[4,64,1,128]{3,2,1,0:T(2,128)(2,1)} %get-tuple-element.29), channel_id=1, source_target_pairs={{0,1},{1,2},{2,3},{3,4},{4,5},{5,6},{6,7},{8,9},{9,10},{10,11},{11... | collective-permute-start | bytes 196616 | tf_op jit(solution)/shard_map/ppermute | solution.py:21
  49.5 3.3 %copy-start.10 = (bf16[3,1,1,128,128]{4,3,0,2,1:T(8,128)(2,1)S(1)}, bf16[3,1,1,128,128]{4,3,0,2,1:T(8,128)(2,1)}, u32[]{:S(2)}) copy-start(bf16[3,1,1,128,128]{4,3,0,2,1:T(8,128)(2,1)} %copy.19) | copy-start | bytes 294916
  52.8 1.0 copy-start.9
  53.8 1.2 copy-start.1
  53.8 1.5 %copy-start.2 = (bf16[2,64,32,128]{3,2,1,0:T(8,128)(2,1)S(1)}, bf16[2,64,32,128]{3,2,1,0:T(8,128)(2,1)}, u32[]{:S(2)}) copy-start(bf16[2,64,32,128]{3,2,1,0:T(8,128)(2,1)} %get-tuple-element.10) | copy-start | bytes 3145732
  53.8 1.8 %copy-start.3 = (bf16[2,64,32,128]{3,2,1,0:T(8,128)(2,1)S(1)}, bf16[2,64,32,128]{3,2,1,0:T(8,128)(2,1)}, u32[]{:S(2)}) copy-start(bf16[2,64,32,128]{3,2,1,0:T(8,128)(2,1)} %get-tuple-element.11) | copy-start | bytes 3145732
  53.8 2.1 %copy-start.4 = (bf16[2,64,32,128]{3,2,1,0:T(8,128)(2,1)S(1)}, bf16[2,64,32,128]{3,2,1,0:T(8,128)(2,1)}, u32[]{:S(2)}) copy-start(bf16[2,64,32,128]{3,2,1,0:T(8,128)(2,1)} %get-tuple-element.12) | copy-start | bytes 3145732
  62.5 1.2 copy-start.6
  62.5 1.5 %copy-start.8 = (bf16[2,64,32,128]{3,2,1,0:T(8,128)(2,1)S(1)}, bf16[2,64,32,128]{3,2,1,0:T(8,128)(2,1)}, u32[]{:S(2)}) copy-start(bf16[2,64,32,128]{3,2,1,0:T(8,128)(2,1)} %copy-done.7) | copy-start | bytes 3145732
  68.4 1.0 copy-start.11
  70.6 14.1 %copy-start.12 = (bf16[3,128,16]{1,2,0:T(8,128)(2,1)S(1)}, bf16[3,128,16]{1,2,0:T(8,128)(2,1)}, u32[]{:S(2)}) copy-start(bf16[3,128,16]{1,2,0:T(8,128)(2,1)} %param.6) | copy-start | bytes 36868
  71.9 30.2 %all-to-all-start = ((bf16[1,64,32,128]{3,2,0,1:T(8,128)(2,1)}), bf16[1,64,32,128]{3,2,0,1:T(8,128)(2,1)S(1)}, u32[]{:S(2)}, u32[]{:S(2)}) async-start(bf16[1,64,32,128]{3,2,0,1:T(8,128)(2,1)} %fusion.15), calls=%async_computation | async-start | bytes 1048576 | tf_op jit(solution)/shard_map/all_to_all | solution.py:67
  104.9 23.8 %all-to-all-start.1 = ((f32[256,1,192]{2,1,0:T(1,128)}), f32[256,1,192]{2,1,0:T(1,128)S(1)}, u32[]{:S(2)}, u32[]{:S(2)}) async-start(f32[256,1,192]{2,1,0:T(1,128)} %all_to_all.22), calls=%async_computation.1 | async-start | bytes 524288 | tf_op jit(solution)/shard_map/all_to_all | solution.py:81
where the time goes:
time: 130 us
  starting transfers between devices  32 us (25%)
  blocking collectives  27.7 us (21%)
  waiting for transfers between devices  25.6 us (20%)
  local copies, waits for them, and re-layouts  17.5 us (13%)
  other arithmetic  13.8 us (11%)
  matrix products  11.9 us (9%)
    all_gather x1, blocking collectives, local(): lax.all_gather(conv_weight, 'fsdp', axis=4, tiled=True)  15 us
    all_to_all x1, waiting for transfers between devices, local(): lax.all_to_all(jnp.stack(grad_terms).reshape(parts, -1), ('tm', 'fsdp'),...  13.9 us
    all_to_all x1, starting transfers between devices, local(): lax.all_to_all(pool_pairs(hidden), 'tm', split_axis=1, concat_axis=0, til...  12.8 us
    all_gather x1, blocking collectives, local(): lax.all_gather(mix_weight, 'fsdp', axis=2, tiled=True)  12.7 us
    dot_general x9, matrix products, local(): accum = accum + jnp.dot(stacked, kernel, preferred_element_type=jnp.float32)  9.18 us
    all_to_all x1, starting transfers between devices, local(): lax.all_to_all(jnp.stack(grad_terms).reshape(parts, -1), ('tm', 'fsdp'),...  8.54 us
    concatenate x5, other arithmetic, local(): jnp.concatenate([padded[step:step + count_frames, row_tap:row_tap + heigh...  7.93 us
    unnamed x36, local copies, waits for them, and re-layouts  7.4 us
  transfers between devices with their start and end apart: 5, of which 3 were waited for; matrix products, arithmetic and copies ran while one was open for 6% of the time, Pallas kernels for 0%

commit v1 on v0

--- a/solution.py
+++ b/solution.py
@@ -64,7 +64,11 @@
             kernel = full_conv[:, row_tap, col_tap].reshape(3 * channels, channels)
             accum = accum + jnp.dot(stacked, kernel, preferred_element_type=jnp.float32)
     hidden = jax.nn.silu(accum).astype(jnp.bfloat16).reshape(count_frames, height, width, channels)
-    pooled = lax.all_to_all(pool_pairs(hidden), "tm", split_axis=1, concat_axis=0, tiled=True)
+    own = pool_pairs(hidden)
+    count_2 = lax.axis_size("tm")
+    blocks = jnp.stack(jnp.split(own, count_2, axis=1), axis=0)
+    blocks = lax.all_to_all(blocks, "tm", split_axis=0, concat_axis=0)
+    pooled = jnp.concatenate(blocks, axis=0)
     branch = pooled.astype(jnp.float32).reshape(-1, channels)
     flat_cot = cotangent.reshape(-1, channels)
     grad_terms = []

time: 130 us -> 149 us (1.15)
  local copies, waits for them, and re-layouts: 17.5 us -> 36.9 us
    unnamed x36 -> x67, local copies, waits for them, and re-layouts: 7.4 us -> 26.2 us
  transfers between devices with their start and end apart: 5 -> 5, of which waited for: 3 -> 3; matrix products, arithmetic and copies ran while one was open for 6% -> 5% of each run, Pallas kernels for 0% -> 0%
where the time goes in v1:
time: 149 us; the launch traced here: 148 us
  local copies, waits for them, and re-layouts  36.9 us (25%)
  starting transfers between devices  32 us (21%)
  blocking collectives  27.7 us (19%)
  waiting for transfers between devices  25.6 us (17%)
  other arithmetic  13 us (9%)
  matrix products  11.9 us (8%)
    unnamed x67, local copies, waits for them, and re-layouts  26.2 us
    all_gather x1, blocking collectives, local(): lax.all_gather(conv_weight, 'fsdp', axis=4, tiled=True)  15 us
    all_to_all x1, waiting for transfers between devices, local(): lax.all_to_all(jnp.stack(grad_terms).reshape(parts, -1), ('tm', 'fsdp'),...  13.9 us
    all_to_all x1, starting transfers between devices, local(): blocks = lax.all_to_all(blocks, 'tm', split_axis=0, concat_axis=0)  12.8 us
    all_gather x1, blocking collectives, local(): lax.all_gather(mix_weight, 'fsdp', axis=2, tiled=True)  12.7 us
    dot_general x9, matrix products, local(): accum = accum + jnp.dot(stacked, kernel, preferred_element_type=jnp.float32)  9.18 us
    all_to_all x1, starting transfers between devices, local(): lax.all_to_all(jnp.stack(grad_terms).reshape(parts, -1), ('tm', 'fsdp'),...  8.53 us
    concatenate x5, other arithmetic, local(): jnp.concatenate([padded[step:step + count_frames, row_tap:row_tap + heigh...  7.93 us
  transfers between devices with their start and end apart: 5, of which 3 were waited for; matrix products, arithmetic and copies ran while one was open for 5% of the time, Pallas kernels for 0%

profile of v1, /device:TPU:1, one launch (start us, length us, event | category | flops | bytes accessed | tf_op | source)
XLA Modules:
  0.0 148.1 jit_solution(18104271132035608237)
XLA Ops:
  0.7 4.1 %collective-permute-start = (bf16[2,64,32,128]{3,2,1,0:T(8,128)(2,1)}, bf16[2,64,32,128]{3,2,1,0:T(8,128)(2,1)S(1)}, u32[]{:S(2)}, u32[]{:S(2)}) collective-permute-start(bf16[2,64,32,128]{3,2,1,0:T(8,128)(2,1)} %param.4), channel_id=1, source_target_pairs={{0,8},{8,16},{16,24},{24,32},{32,40},{40,48},{48,56},{56,64},{64,7... | collective-permute-start | bytes 3145736 | tf_op jit(solution)/shard_map/ppermute | solution.py:10
  4.8 15.0 %all_gather.6 = bf16[3,3,3,128,128]{3,4,2,1,0:T(8,128)(2,1)S(1)} all-gather(bf16[3,3,3,128,16]{3,4,2,1,0:T(8,128)(2,1)} %param.5), channel_id=1, replica_groups=mesh['tm'=32,'fsdp'=8] {'fsdp'}, dimensions={4}, use_global_device_ids=true | all-gather | bytes 995328 | tf_op jit(solution)/shard_map/all_gather | solution.py:41
  19.8 7.0 %collective-permute-done = bf16[2,64,32,128]{3,2,1,0:T(8,128)(2,1)S(1)} collective-permute-done((bf16[2,64,32,128]{3,2,1,0:T(8,128)(2,1)}, bf16[2,64,32,128]{3,2,1,0:T(8,128)(2,1)S(1)}, u32[]{:S(2)}, u32[]{:S(2)}) %collective-permute-start) | collective-permute-done | bytes 1048608 | tf_op jit(solution)/shard_map/ppermute | solution.py:10
  28.0 3.4 %collective-permute-start.2 = (bf16[4,64,1,128]{3,2,1,0:T(2,128)(2,1)}, bf16[4,64,1,128]{3,2,1,0:T(2,128)(2,1)S(1)}, u32[]{:S(2)}, u32[]{:S(2)}) collective-permute-start(bf16[4,64,1,128]{3,2,1,0:T(2,128)(2,1)} %get-tuple-element.30), channel_id=1, source_target_pairs={{1,0},{2,1},{3,2},{4,3},{5,4},{6,5},{7,6},{9,8},{10,9},{11,10},{12... | collective-permute-start | bytes 196616 | tf_op jit(solution)/shard_map/ppermute | solution.py:23
  31.5 3.1 %collective-permute-start.1 = (bf16[4,64,1,128]{3,2,1,0:T(2,128)(2,1)}, bf16[4,64,1,128]{3,2,1,0:T(2,128)(2,1)S(1)}, u32[]{:S(2)}, u32[]{:S(2)}) collective-permute-start(bf16[4,64,1,128]{3,2,1,0:T(2,128)(2,1)} %get-tuple-element.29), channel_id=1, source_target_pairs={{0,1},{1,2},{2,3},{3,4},{4,5},{5,6},{6,7},{8,9},{9,10},{10,11},{11... | collective-permute-start | bytes 196616 | tf_op jit(solution)/shard_map/ppermute | solution.py:21
  35.3 1.6 %copy.81 = bf16[3,1,1,128,128]{4,3,0,2,1:T(8,128)(2,1)} copy(bf16[3,1,1,128,128]{3,4,2,1,0:T(8,128)(2,1)} %get-tuple-element.39) | data formatting | bytes 196608
  38.4 1.0 copy.88
  39.4 1.6 %copy.89 = bf16[3,1,1,128,128]{4,3,0,2,1:T(8,128)(2,1)} copy(bf16[3,1,1,128,128]{3,4,2,1,0:T(8,128)(2,1)} %get-tuple-element.31) | data formatting | bytes 196608
  41.1 1.5 %fusion.7 = bf16[4,66,34,128]{3,2,1,0:T(8,128)(2,1)S(1)} fusion(bf16[4,64,1,128]{3,2,1,0:T(2,128)(2,1)S(1)} %collective-permute-done.2, bf16[4,64,32,128]{3,2,1,0:T(8,128)(2,1)S(1)} %constant_dynamic-update-slice_fusion, bf16[4,64,1,128]{3,2,1,0:T(2,128)(2,1)S(1)} %collective-permute-done.1), kind=kLoop, calls=%fused_computation.30 | loop fusion | flops 13787136 | bytes 4526080 | tf_op jit(solution)/shard_map/concatenate | solution.py:19
  42.6 6.9 %fusion.18 = (bf16[2,64,32,128]{3,2,1,0:T(8,128)(2,1)S(1)}, bf16[2,64,32,128]{3,2,1,0:T(8,128)(2,1)S(1)}, bf16[2,64,32,128]{3,2,1,0:T(8,128)(2,1)S(1)}, bf16[2,6...) fusion(bf16[4,66,34,128]{3,2,1,0:T(8,128)(2,1)S(1)} %fusion.7), kind=kLoop, calls=%fused_computation.125 | loop fusion | bytes 37748736 | tf_op jit(solution)/shard_map/slice | solution.py:54
  49.5 3.3 %pad_maximum_fusion.2 = (bf16[2,64,32,384]{3,2,1,0:T(8,128)(2,1)S(1)}, bf16[2,64,32,384]{3,2,1,0:T(8,128)(2,1)S(1)}) fusion(bf16[2,64,32,128]{3,2,1,0:T(8,128)(2,1)} %get-tuple-element.16, bf16[2,64,32,128]{3,2,1,0:T(8,128)(2,1)} %get-tuple-element.17, bf16[2,64,32,128]{3,2,1,0:T(8,128)(2,1)} %get-tuple-element.18, ...), kind=kLoop, calls=%fused_computation.19 | loop fusion | flops 18874368 | bytes 12582912 | tf_op jit(solution)/shard_map/concatenate | solution.py:52
  53.9 1.1 convolution_add_fusion.7
  57.8 2.1 %fusion.10 = (bf16[2,64,32,128]{3,2,1,0:T(8,128)(2,1)S(1)}, bf16[2,64,32,128]{3,2,1,0:T(8,128)(2,1)S(1)}, bf16[2,64,32,128]{3,2,1,0:T(8,128)(2,1)S(1)}, bf16[2,6...) fusion(bf16[4,64,32,128]{3,2,1,0:T(8,128)(2,1)S(1)} %constant_dynamic-update-slice_fusion, ...), kind=kLoop, calls=%fused_computation.44 | loop fusion | flops 8388608 | bytes 8650752 | tf_op jit(solution)/shard_map/concatenate | solution.py:19
  60.0 2.5 %fusion.1 = (bf16[2,64,32,384]{3,2,1,0:T(8,128)(2,1)S(1)}, bf16[2,64,32,384]{3,2,1,0:T(8,128)(2,1)S(1)}) fusion(bf16[4,64,1,128]{3,2,1,0:T(2,128)(2,1)S(1)} %collective-permute-done.2, bf16[4,64,32,128]{3,2,1,0:T(8,128)(2,1)S(1)} %constant_dynamic-update-slice_fusion, bf16[2,64,32,128]{3,2,1,0:T(8,128)(2,1)S(1)} %get-tuple-element.21, ...), kind=kLoop, calls=%fused_computation.16 | loop fusion | flops 25165824 | bytes 12713984 | tf_op jit(solution)/shard_map/concatenate | solution.py:52
  66.5 1.0 convolution_add_fusion.2
  68.4 1.0 convolution_add_fusion.1
  69.5 1.1 multiply_convert_fusion
  90.5 12.8 %all-to-all-start = ((bf16[32,1,2,32,128]{4,3,2,1,0:T(8,128)(2,1)}), bf16[32,1,2,32,128]{4,3,2,1,0:T(8,128)(2,1)S(1)}, u32[]{:S(2)}, u32[]{:S(2)}) async-start(bf16[32,1,2,32,128]{4,3,2,1,0:T(8,128)(2,1)} %constant_dynamic-update-slice_fusion.2), calls=%async_computation | async-start | bytes 1048576 | tf_op jit(solution)/shard_map/all_to_all | solution.py:70
  103.4 12.7 %all_gather.7 = bf16[3,128,128]{1,2,0:T(8,128)(2,1)S(1)} all-gather(bf16[3,128,16]{1,2,0:T(8,128)(2,1)S(1)} %copy-done.12), channel_id=1, replica_groups=mesh['tm'=32,'fsdp'=8] {'fsdp'}, dimensions={2}, use_global_device_ids=true | all-gather | bytes 110592 | tf_op jit(solution)/shard_map/all_gather | solution.py:42
  116.0 4.7 %all-to-all-done = bf16[32,1,2,32,128]{4,3,2,1,0:T(8,128)(2,1)S(1)} async-done(((bf16[32,1,2,32,128]{4,3,2,1,0:T(8,128)(2,1)}), bf16[32,1,2,32,128]{4,3,2,1,0:T(8,128)(2,1)S(1)}, u32[]{:S(2)}, u32[]{:S(2)}) %all-to-all-start) | async-done | bytes 524320 | tf_op jit(solution)/shard_map/all_to_all | solution.py:70
  122.3 1.1 all_to_all.12
  123.5 8.5 %all-to-all-start.1 = ((f32[256,1,192]{2,1,0:T(1,128)}), f32[256,1,192]{2,1,0:T(1,128)S(1)}, u32[]{:S(2)}, u32[]{:S(2)}) async-start(f32[256,1,192]{2,1,0:T(1,128)} %all_to_all.12), calls=%async_computation.1 | async-start | bytes 524288 | tf_op jit(solution)/shard_map/all_to_all | solution.py:85
  132.3 1.1 fusion.8
  133.4 13.9 %all-to-all-done.1 = f32[256,1,192]{2,1,0:T(1,128)S(1)} async-done(((f32[256,1,192]{2,1,0:T(1,128)}), f32[256,1,192]{2,1,0:T(1,128)S(1)}, u32[]{:S(2)}, u32[]{:S(2)}) %all-to-all-start.1) | async-done | bytes 196640 | tf_op jit(solution)/shard_map/all_to_all | solution.py:85
  (88 shorter events, 34.7 us)
Async XLA Ops:
  0.6 120.7 %copy-start = (bf16[32,2,32,128]{3,2,1,0:T(8,128)(2,1)S(1)}, bf16[32,2,32,128]{3,2,1,0:T(8,128)(2,1)}, u32[]{:S(2)}) copy-start(bf16[32,2,32,128]{3,2,1,0:T(8,128)(2,1)} %param.7) | copy-start | bytes 1572868
  0.6 26.3 %copy-start.5 = (bf16[2,64,32,128]{3,2,1,0:T(8,128)(2,1)S(1)}, bf16[2,64,32,128]{3,2,1,0:T(8,128)(2,1)}, u32[]{:S(2)}) copy-start(bf16[2,64,32,128]{3,2,1,0:T(8,128)(2,1)} %param.4) | copy-start | bytes 3145732
  0.7 26.2 %collective-permute-start = (bf16[2,64,32,128]{3,2,1,0:T(8,128)(2,1)}, bf16[2,64,32,128]{3,2,1,0:T(8,128)(2,1)S(1)}, u32[]{:S(2)}, u32[]{:S(2)}) collective-permute-start(bf16[2,64,32,128]{3,2,1,0:T(8,128)(2,1)} %param.4), channel_id=1, source_target_pairs={{0,8},{8,16},{16,24},{24,32},{32,40},{40,48},{48,56},{56,64},{64,7... | collective-permute-start | bytes 3145736 | tf_op jit(solution)/shard_map/ppermute | solution.py:10
  26.9 8.5 %copy-start.7 = (bf16[2,64,32,128]{3,2,1,0:T(8,128)(2,1)}, bf16[2,64,32,128]{3,2,1,0:T(8,128)(2,1)S(1)}, u32[]{:S(2)}) copy-start(bf16[2,64,32,128]{3,2,1,0:T(8,128)(2,1)S(1)} %collective-permute-done) | copy-start | bytes 3145732
  28.0 13.0 %collective-permute-start.2 = (bf16[4,64,1,128]{3,2,1,0:T(2,128)(2,1)}, bf16[4,64,1,128]{3,2,1,0:T(2,128)(2,1)S(1)}, u32[]{:S(2)}, u32[]{:S(2)}) collective-permute-start(bf16[4,64,1,128]{3,2,1,0:T(2,128)(2,1)} %get-tuple-element.30), channel_id=1, source_target_pairs={{1,0},{2,1},{3,2},{4,3},{5,4},{6,5},{7,6},{9,8},{10,9},{11,10},{12... | collective-permute-start | bytes 196616 | tf_op jit(solution)/shard_map/ppermute | solution.py:23
  31.5 9.6 %collective-permute-start.1 = (bf16[4,64,1,128]{3,2,1,0:T(2,128)(2,1)}, bf16[4,64,1,128]{3,2,1,0:T(2,128)(2,1)S(1)}, u32[]{:S(2)}, u32[]{:S(2)}) collective-permute-start(bf16[4,64,1,128]{3,2,1,0:T(2,128)(2,1)} %get-tuple-element.29), channel_id=1, source_target_pairs={{0,1},{1,2},{2,3},{3,4},{4,5},{5,6},{6,7},{8,9},{9,10},{10,11},{11... | collective-permute-start | bytes 196616 | tf_op jit(solution)/shard_map/ppermute | solution.py:21
  49.5 3.3 %copy-start.10 = (bf16[3,1,1,128,128]{4,3,0,2,1:T(8,128)(2,1)S(1)}, bf16[3,1,1,128,128]{4,3,0,2,1:T(8,128)(2,1)}, u32[]{:S(2)}) copy-start(bf16[3,1,1,128,128]{4,3,0,2,1:T(8,128)(2,1)} %copy.81) | copy-start | bytes 294916
  52.8 1.0 copy-start.9
  53.8 1.2 copy-start.1
  53.8 1.5 %copy-start.2 = (bf16[2,64,32,128]{3,2,1,0:T(8,128)(2,1)S(1)}, bf16[2,64,32,128]{3,2,1,0:T(8,128)(2,1)}, u32[]{:S(2)}) copy-start(bf16[2,64,32,128]{3,2,1,0:T(8,128)(2,1)} %get-tuple-element.10) | copy-start | bytes 3145732
  53.8 1.8 %copy-start.3 = (bf16[2,64,32,128]{3,2,1,0:T(8,128)(2,1)S(1)}, bf16[2,64,32,128]{3,2,1,0:T(8,128)(2,1)}, u32[]{:S(2)}) copy-start(bf16[2,64,32,128]{3,2,1,0:T(8,128)(2,1)} %get-tuple-element.11) | copy-start | bytes 3145732
  53.8 2.1 %copy-start.4 = (bf16[2,64,32,128]{3,2,1,0:T(8,128)(2,1)S(1)}, bf16[2,64,32,128]{3,2,1,0:T(8,128)(2,1)}, u32[]{:S(2)}) copy-start(bf16[2,64,32,128]{3,2,1,0:T(8,128)(2,1)} %get-tuple-element.12) | copy-start | bytes 3145732
  62.5 1.2 copy-start.6
  62.5 1.5 %copy-start.8 = (bf16[2,64,32,128]{3,2,1,0:T(8,128)(2,1)S(1)}, bf16[2,64,32,128]{3,2,1,0:T(8,128)(2,1)}, u32[]{:S(2)}) copy-start(bf16[2,64,32,128]{3,2,1,0:T(8,128)(2,1)} %copy-done.7) | copy-start | bytes 3145732
  68.4 1.0 copy-start.11
  70.9 32.5 %copy-start.12 = (bf16[3,128,16]{1,2,0:T(8,128)(2,1)S(1)}, bf16[3,128,16]{1,2,0:T(8,128)(2,1)}, u32[]{:S(2)}) copy-start(bf16[3,128,16]{1,2,0:T(8,128)(2,1)} %param.6) | copy-start | bytes 36868
  90.5 30.2 %all-to-all-start = ((bf16[32,1,2,32,128]{4,3,2,1,0:T(8,128)(2,1)}), bf16[32,1,2,32,128]{4,3,2,1,0:T(8,128)(2,1)S(1)}, u32[]{:S(2)}, u32[]{:S(2)}) async-start(bf16[32,1,2,32,128]{4,3,2,1,0:T(8,128)(2,1)} %constant_dynamic-update-slice_fusion.2), calls=%async_computation | async-start | bytes 1048576 | tf_op jit(solution)/shard_map/all_to_all | solution.py:70
  123.5 23.8 %all-to-all-start.1 = ((f32[256,1,192]{2,1,0:T(1,128)}), f32[256,1,192]{2,1,0:T(1,128)S(1)}, u32[]{:S(2)}, u32[]{:S(2)}) async-start(f32[256,1,192]{2,1,0:T(1,128)} %all_to_all.12), calls=%async_computation.1 | async-start | bytes 524288 | tf_op jit(solution)/shard_map/all_to_all | solution.py:85
